TPU v7x, 32 devices: a whole 2x2x4 slice. The times are simulated.
32 devices in a mesh: term: 8 (over y, x, core), topic: 4 (over z).
Axes of the slice: x: 2, y: 2, z: 4, core: 2. Of those that a mesh axis runs over, the one named last changes fastest.
Arguments:
- factor: bfloat16 [65536, 512], P('term', 'topic'), may hold values from 1e-06 to 0.05, as said below
- tile_values: bfloat16 [65536, 128], P('term'), may hold values from 0.049804688 to 1
- tile_docs: int32 [8, 128], P('term'), may hold values from 0 to 127, as said below
- codes: float32 [512, 128], P('topic', 'term'), may hold values from 0.1 to 2
- gram_stat: float32 [512, 512], P('topic', 'term'), may hold values from 0 to 4
- data_stat: float32 [65536, 512], P('term', 'topic'), may hold values from 0 to 0.4
Outputs:
- codes_out: float32 [512, 128], P('topic', 'term')
- gram_new: float32 [512, 512], P('topic', 'term')
- data_new: float32 [65536, 512], P('term', 'topic')
Inputs may be any that keep to these rules, and one draw needn't show every extreme that they name: `tile_docs`: each row lists 128 different document numbers. `factor`: positive entries.
All inputs are finite; a program needn't handle non-finite values.
Results may differ from a plain program's by a relative error of at most 0.0003.
Values may be sent and summed in bfloat16 or wider, within the bound.
No kernel may reach another device: no remote copies, remote signals or barrier semaphores. Data moves between devices by JAX's collectives and lax.ppermute only.
A program may use at most 128 MiB of HBM per device.

v0:
```python
import jax
import jax.numpy as jnp
from jax import lax
from jax.sharding import PartitionSpec as P

ITERS = 3
EPSILON = 1e-06
DECAY = 0.5


def contract_rows(left, right):
    return lax.dot_general(
        left, right, (((0,), (0,)), ((), ())), preferred_element_type=jnp.float32
    )


def apply_gram(gram_rows, current):
    return jnp.dot(
        gram_rows,
        lax.all_gather(current, "topic", axis=0, tiled=True),
        precision=lax.Precision.HIGHEST,
        preferred_element_type=jnp.float32,
    )


def per_device(factor, tile_values, tile_docs, codes, gram_stat, data_stat):
    term_count = lax.axis_size("term")
    documents = codes.shape[1] * term_count
    onehot = (tile_docs[0][:, None] == jnp.arange(documents, dtype=jnp.int32)[None, :]).astype(
        jnp.bfloat16
    )
    batch = jnp.dot(tile_values, onehot, preferred_element_type=jnp.float32).astype(jnp.bfloat16)
    partial_data = contract_rows(factor, batch)
    data_share = lax.psum_scatter(partial_data, "term", scatter_dimension=1, tiled=True)
    row_block = lax.all_to_all(factor, "topic", split_axis=0, concat_axis=1, tiled=True)
    gram_part = lax.psum_scatter(
        contract_rows(row_block, row_block), "topic", scatter_dimension=0, tiled=True
    )
    gram_rows = lax.psum(gram_part, "term")
    current = codes
    for update in range(ITERS):
        current = current * data_share / (apply_gram(gram_rows, current) + EPSILON)
    outer = lax.dot_general(
        current,
        lax.all_gather(current, "topic", axis=0, tiled=True),
        (((1,), (1,)), ((), ())),
        precision=lax.Precision.HIGHEST,
        preferred_element_type=jnp.float32,
    )
    outer_share = lax.psum_scatter(outer, "term", scatter_dimension=1, tiled=True)
    gram_new = DECAY * gram_stat + outer_share / documents
    code_row = lax.all_gather(current, "term", axis=1, tiled=True)
    widened = batch.astype(jnp.float32)
    product = lax.dot_general(
        widened,
        code_row,
        (((1,), (1,)), ((), ())),
        precision=lax.Precision.HIGHEST,
        preferred_element_type=jnp.float32,
    )
    data_new = DECAY * data_stat + product / documents
    return (current, gram_new, data_new)


def solution(mesh):
    placed = (
        P("term", "topic"),
        P("term", None),
        P("term", None),
        P("topic", "term"),
        P("topic", "term"),
        P("term", "topic"),
    )
    return jax.shard_map(
        per_device,
        mesh=mesh,
        in_specs=placed,
        out_specs=(P("topic", "term"), P("topic", "term"), P("term", "topic")),
        check_vma=False,
    )
```

profile of v0, /device:TPU:0, one launch (start us, length us, event | category | flops | bytes accessed | tf_op | source)
XLA Modules:
  0.0 284.7 jit_solution(639582228280729309)
XLA Ops:
  7.2 0.0 copy-start
  7.2 0.0 reduce-scatter.6.cloned.1.call-start
  7.2 54.8 %all_to_all.19 = bf16[4,2048,128]{2,1,0:T(8,128)(2,1)} all-to-all(bf16[4,2048,128]{2,1,0:T(8,128)(2,1)} %bitcast.21), channel_id=1, replica_groups=mesh['term'=8,'topic'=4] {'topic'}, dimensions={0} | all-to-all | bytes 4194304 | tf_op jit(solution)/shard_map/all_to_all | solution.py:35
  62.0 3.9 %copy.9 = bf16[2048,4,128]{0,2,1:T(8,128)(2,1)} copy(bf16[2048,4,128]{2,0,1:T(8,128)(2,1)} %bitcast.22) | data formatting | bytes 4194304 | tf_op jit(solution)/shard_map/all_to_all | solution.py:35
  66.0 0.0 copy-start.6
  66.0 4.5 %fusion.7 = f32[512,512]{1,0:T(8,128)} fusion(bf16[2048,512]{0,1:T(8,128)(2,1)} %bitcast.23), kind=kOutput, calls=%fused_computation.14 | convolution fusion | flops 1073741824 | bytes 3145728 | tf_op jit(solution)/shard_map/dot_general | solution.py:12
  70.5 0.0 reduce-scatter.6.cloned.1.call-update
  70.5 0.0 reduce-scatter.4.cloned.1.call-start
  70.5 0.0 copy-done
  70.5 0.0 copy-done.6
  70.6 0.0 copy-start.2
  70.6 0.8 convolution_convert_fusion
  71.4 0.0 copy-start.1
  71.4 1.3 copy-done.1
  72.7 0.0 copy-done.2
  72.7 0.0 copy-start.5
  72.7 1.3 convolution_bitcast_fusion
  74.1 0.0 reduce-scatter.4.cloned.1.call-update
  74.1 0.0 all-reduce.2.cloned.1.call-start
  74.1 23.0 %reduce-scatter.6.cloned.1.call-done = f32[128,512]{1,0:T(8,128)} async-done(((f32[512,512]{1,0:T(8,128)}), f32[128,512]{1,0:T(8,128)}) %reduce-scatter.6.cloned.1.call-update) | async-done | bytes 262160 | tf_op jit(solution)/shard_map/reduce_scatter | solution.py:36
  97.2 0.0 all-reduce.2.cloned.1.call-update
  97.2 0.0 reduce-scatter.8.cloned.1.call-start
  97.2 0.0 copy-done.5
  97.3 13.1 %all_gather.15 = f32[512,16]{0,1:T(8,128)S(1)} all-gather(f32[128,16]{0,1:T(8,128)S(1)} %copy-done.5), channel_id=1, replica_groups=mesh['term'=8,'topic'=4] {'topic'}, dimensions={0}, use_global_device_ids=true | all-gather | bytes 40960 | tf_op jit(solution)/shard_map/all_gather | solution.py:20
  110.4 22.4 %reduce-scatter.4.cloned.1.call-done = f32[128,16]{0,1:T(8,128)} async-done(((f32[128,128]{0,1:T(8,128)}), f32[128,16]{0,1:T(8,128)}) %reduce-scatter.4.cloned.1.call-update) | async-done | bytes 8208 | tf_op jit(solution)/shard_map/reduce_scatter | solution.py:34
  132.8 57.0 %all-reduce.2.cloned.1.call-done = f32[128,512]{1,0:T(8,128)} async-done(((f32[128,512]{1,0:T(8,128)}), f32[128,512]{1,0:T(8,128)}) %all-reduce.2.cloned.1.call-update) | async-done | bytes 262160 | tf_op jit(solution)/shard_map/psum | solution.py:39
  189.8 1.3 fusion.3
  191.0 13.2 %all_gather.16 = f32[512,16]{0,1:T(8,128)S(1)} all-gather(f32[128,16]{0,1:T(8,128)S(1)} %fusion.3), channel_id=1, replica_groups=mesh['term'=8,'topic'=4] {'topic'}, dimensions={0}, use_global_device_ids=true | all-gather | bytes 40960 | tf_op jit(solution)/shard_map/all_gather | solution.py:20
  204.2 1.3 fusion.2
  205.5 13.1 %all_gather.17 = f32[512,16]{0,1:T(8,128)S(1)} all-gather(f32[128,16]{0,1:T(8,128)S(1)} %fusion.2), channel_id=1, replica_groups=mesh['term'=8,'topic'=4] {'topic'}, dimensions={0}, use_global_device_ids=true | all-gather | bytes 40960 | tf_op jit(solution)/shard_map/all_gather | solution.py:20
  218.6 1.3 fusion.1
  219.9 0.0 copy-start.3
  219.9 8.6 %all_gather.19 = f32[128,128]{0,1:T(8,128)S(1)} all-gather(f32[128,16]{0,1:T(8,128)S(1)} %fusion.1), channel_id=1, replica_groups=mesh['term'=8,'topic'=4] {'term'}, dimensions={1}, use_global_device_ids=true | all-gather | bytes 73728 | tf_op jit(solution)/shard_map/all_gather | solution.py:52
  228.6 13.1 %all_gather.18 = f32[512,16]{0,1:T(8,128)S(1)} all-gather(f32[128,16]{0,1:T(8,128)S(1)} %fusion.1), channel_id=1, replica_groups=mesh['term'=8,'topic'=4] {'topic'}, dimensions={0}, use_global_device_ids=true | all-gather | bytes 40960 | tf_op jit(solution)/shard_map/all_gather | solution.py:45
  241.7 1.3 fusion.8
  243.0 0.0 reduce-scatter.8.cloned.1.call-update
  243.0 0.0 copy-start.4
  243.0 7.4 %fusion = f32[8192,128]{1,0:T(8,128)} fusion(bf16[128,8192]{1,0:T(8,128)(2,1)} %copy-done.1, f32[128,128]{0,1:T(8,128)S(1)} %all_gather.19, f32[8192,128]{1,0:T(8,128)} %param.11), kind=kOutput, calls=%fused_computation.1 | convolution fusion | flops 1613758464 | bytes 10551296 | tf_op jit(solution)/shard_map/dot_general | solution.py:54
  250.4 0.0 copy-done.3
  250.4 26.5 %reduce-scatter.8.cloned.1.call-done = f32[128,64]{0,1:T(8,128)} async-done(((f32[128,512]{0,1:T(8,128)}), f32[128,64]{0,1:T(8,128)}) %reduce-scatter.8.cloned.1.call-update) | async-done | bytes 32784 | tf_op jit(solution)/shard_map/reduce_scatter | solution.py:50
  276.8 0.0 copy-done.4
  276.8 1.4 multiply_add_fusion
Async XLA Ops:
  7.2 63.4 %copy-start = (bf16[8192,128]{1,0:T(8,128)(2,1)S(1)}, bf16[8192,128]{1,0:T(8,128)(2,1)}, u32[]{:S(2)}) copy-start(bf16[8192,128]{1,0:T(8,128)(2,1)} %param.7) | copy-start | bytes 6291460
  7.2 90.0 %reduce-scatter.6.cloned.1.call-start = ((), (), s32[]{:S(2)}) async-start(), calls=%async_computation.5 | async-start | bytes 1310720 | tf_op jit(solution)/shard_map/reduce_scatter | solution.py:36
  66.0 4.6 %copy-start.6 = (s32[1,128]{1,0:T(1,128)S(1)}, s32[1,128]{1,0:T(1,128)}, u32[]{:S(2)}) copy-start(s32[1,128]{1,0:T(1,128)} %param.8) | copy-start | bytes 1540
  70.5 62.3 %reduce-scatter.4.cloned.1.call-start = ((), (), s32[]{:S(2)}) async-start(), calls=%async_computation.4 | async-start | bytes 73728 | tf_op jit(solution)/shard_map/reduce_scatter | solution.py:34
  70.6 2.2 copy-start.2
  71.4 1.3 copy-start.1
  72.7 24.5 %copy-start.5 = (f32[128,16]{0,1:T(8,128)S(1)}, f32[128,16]{0,1:T(8,128)}, u32[]{:S(2)}) copy-start(f32[128,16]{0,1:T(8,128)} %param.9) | copy-start | bytes 24580
  74.1 115.7 %all-reduce.2.cloned.1.call-start = ((), (), s32[]{:S(2)}) async-start(), calls=%async_computation.6 | async-start | bytes 524288 | tf_op jit(solution)/shard_map/psum | solution.py:39
  97.2 179.6 %reduce-scatter.8.cloned.1.call-start = ((), (), s32[]{:S(2)}) async-start(), calls=%async_computation.7 | async-start | bytes 294912 | tf_op jit(solution)/shard_map/reduce_scatter | solution.py:50
  219.9 30.4 %copy-start.3 = (f32[128,16]{0,1:T(8,128)}, f32[128,16]{0,1:T(8,128)S(1)}, u32[]{:S(2)}) copy-start(f32[128,16]{0,1:T(8,128)S(1)} %fusion.1) | copy-start | bytes 24580
  243.0 33.8 %copy-start.4 = (f32[128,64]{0,1:T(8,128)S(1)}, f32[128,64]{0,1:T(8,128)}, u32[]{:S(2)}) copy-start(f32[128,64]{0,1:T(8,128)} %param.10) | copy-start | bytes 98308
Sparse Core Ops, SparseCore 0:
  70.6 26.5 reduce-scatter.5
  100.7 31.9 reduce-scatter.3
  135.8 53.8 all-reduce.1
  243.1 33.6 reduce-scatter.7
where the time goes:
time: 285 us
  waiting for transfers between devices  129 us (45%)
  blocking collectives  116 us (41%)
  matrix products  19.1 us (7%)
  between operations  13.9 us (5%)
  local copies, waits for them, and re-layouts  5.32 us (2%)
    psum x1, waiting for transfers between devices, per_device(): gram_rows = lax.psum(gram_part, 'term')  57 us
    all_to_all x1, blocking collectives, per_device(): lax.all_to_all(factor, 'topic', split_axis=0, concat_axis=1, tiled=True)  54.8 us
    all_gather x3, blocking collectives, apply_gram(): lax.all_gather(current, 'topic', axis=0, tiled=True)  39.5 us
    reduce_scatter x1, waiting for transfers between devices, per_device(): lax.psum_scatter(outer, 'term', scatter_dimension=1, tiled=True)  26.5 us
    reduce_scatter x1, waiting for transfers between devices, per_device(): lax.psum_scatter(contract_rows(row_block, row_block), 'topic', scatter_di...  23 us
    reduce_scatter x1, waiting for transfers between devices, per_device(): lax.psum_scatter(partial_data, 'term', scatter_dimension=1, tiled=True)  22.4 us
    all_gather x1, blocking collectives, per_device(): lax.all_gather(current, 'topic', axis=0, tiled=True)  13.1 us
    all_gather x1, blocking collectives, per_device(): code_row = lax.all_gather(current, 'term', axis=1, tiled=True)  8.61 us
  transfers between devices with their start and end apart: 4, of which 4 were waited for; matrix products, arithmetic and copies ran while one was open for 3% of the time, Pallas kernels for 0%

commit v1 on v0

--- a/solution.py
+++ b/solution.py
@@ -36,7 +36,7 @@
     gram_part = lax.psum_scatter(
         contract_rows(row_block, row_block), "topic", scatter_dimension=0, tiled=True
     )
-    gram_rows = lax.psum(gram_part, "term")
+    gram_rows = jnp.sum(lax.all_gather(gram_part, "term"), 0)
     current = codes
     for update in range(ITERS):
         current = current * data_share / (apply_gram(gram_rows, current) + EPSILON)

time: 285 us -> 258 us (0.905)
  waiting for transfers between devices: 129 us -> 99.8 us
    psum x1 -> x0, waiting for transfers between devices: 57 us -> none  [per_device(): gram_rows = lax.psum(gram_part, 'term')]
    reduce_scatter x1, waiting for transfers between devices: 22.4 us -> 35.3 us  [per_device(): lax.psum_scatter(partial_data, 'term', scatter_dimension=1, tiled=True)]
    all_gather x0 -> x1, waiting for transfers between devices: none -> 11.4 us  [per_device(): gram_rows = jnp.sum(lax.all_gather(gram_part, 'term'), 0)]
    reduce_scatter x1, waiting for transfers between devices: 23 us -> 26.6 us  [per_device(): lax.psum_scatter(contract_rows(row_block, row_block), 'topic', scatter_di...]
  transfers between devices with their start and end apart: 4 -> 4, of which waited for: 4 -> 4; matrix products, arithmetic and copies ran while one was open for 3% -> 4% of each run, Pallas kernels for 0% -> 0%
where the time goes in v1:
time: 258 us; the launch traced here: 257 us
  blocking collectives  117 us (45%)
  waiting for transfers between devices  99.8 us (39%)
  matrix products  18.3 us (7%)
  between operations  13.9 us (5%)
  local copies, waits for them, and re-layouts  5.32 us (2%)
  other arithmetic  3.2 us (1%)
    all_to_all x1, blocking collectives, per_device(): lax.all_to_all(factor, 'topic', split_axis=0, concat_axis=1, tiled=True)  54.8 us
    all_gather x3, blocking collectives, apply_gram(): lax.all_gather(current, 'topic', axis=0, tiled=True)  39.5 us
    reduce_scatter x1, waiting for transfers between devices, per_device(): lax.psum_scatter(partial_data, 'term', scatter_dimension=1, tiled=True)  35.3 us
    reduce_scatter x1, waiting for transfers between devices, per_device(): lax.psum_scatter(contract_rows(row_block, row_block), 'topic', scatter_di...  26.6 us
    reduce_scatter x1, waiting for transfers between devices, per_device(): lax.psum_scatter(outer, 'term', scatter_dimension=1, tiled=True)  26.5 us
    all_gather x1, blocking collectives, per_device(): lax.all_gather(current, 'topic', axis=0, tiled=True)  13.1 us
    all_gather x1, waiting for transfers between devices, per_device(): gram_rows = jnp.sum(lax.all_gather(gram_part, 'term'), 0)  11.4 us
    all_gather x1, blocking collectives, per_device(): code_row = lax.all_gather(current, 'term', axis=1, tiled=True)  9.2 us
  transfers between devices with their start and end apart: 4, of which 4 were waited for; matrix products, arithmetic and copies ran while one was open for 4% of the time, Pallas kernels for 0%

profile of v1, /device:TPU:0, one launch (start us, length us, event | category | flops | bytes accessed | tf_op | source)
XLA Modules:
  0.0 257.3 jit_solution(8143036711948958806)
XLA Ops:
  7.2 0.0 copy-start
  7.2 0.0 reduce-scatter.6.cloned.1.call-start
  7.2 54.8 %all_to_all.19 = bf16[4,2048,128]{2,1,0:T(8,128)(2,1)} all-to-all(bf16[4,2048,128]{2,1,0:T(8,128)(2,1)} %bitcast.22), channel_id=1, replica_groups=mesh['term'=8,'topic'=4] {'topic'}, dimensions={0} | all-to-all | bytes 4194304 | tf_op jit(solution)/shard_map/all_to_all | solution.py:35
  62.0 3.9 %copy.9 = bf16[2048,4,128]{0,2,1:T(8,128)(2,1)} copy(bf16[2048,4,128]{2,0,1:T(8,128)(2,1)} %bitcast.23) | data formatting | bytes 4194304 | tf_op jit(solution)/shard_map/all_to_all | solution.py:35
  66.0 0.0 copy-start.6
  66.0 4.5 %fusion.7 = f32[512,512]{1,0:T(8,128)} fusion(bf16[2048,512]{0,1:T(8,128)(2,1)} %bitcast.25), kind=kOutput, calls=%fused_computation.14 | convolution fusion | flops 1073741824 | bytes 3145728 | tf_op jit(solution)/shard_map/dot_general | solution.py:12
  70.4 0.0 reduce-scatter.6.cloned.1.call-update
  70.5 0.0 all-gather.3.cloned.1.call-start
  70.5 26.6 %reduce-scatter.6.cloned.1.call-done = f32[128,512]{1,0:T(8,128)} async-done(((f32[512,512]{1,0:T(8,128)}), f32[128,512]{1,0:T(8,128)}) %reduce-scatter.6.cloned.1.call-update) | async-done | bytes 262160 | tf_op jit(solution)/shard_map/reduce_scatter | solution.py:36
  97.1 0.0 all-gather.3.cloned.1.call-update
  97.2 0.0 reduce-scatter.4.cloned.1.call-start
  97.2 0.0 copy-done
  97.2 0.0 copy-done.6
  97.2 0.0 copy-start.2
  97.3 0.8 convolution_convert_fusion
  98.1 0.0 copy-start.1
  98.1 1.3 copy-done.1
  99.4 0.0 copy-done.2
  99.4 0.0 copy-start.5
  99.4 1.3 convolution_bitcast_fusion
  100.8 0.0 reduce-scatter.4.cloned.1.call-update
  100.8 0.0 reduce-scatter.8.cloned.1.call-start
  100.8 0.0 copy-done.5
  100.8 13.1 %all_gather.23 = f32[512,16]{0,1:T(8,128)S(1)} all-gather(f32[128,16]{0,1:T(8,128)S(1)} %copy-done.5), channel_id=1, replica_groups=mesh['term'=8,'topic'=4] {'topic'}, dimensions={0}, use_global_device_ids=true | all-gather | bytes 40960 | tf_op jit(solution)/shard_map/all_gather | solution.py:20
  114.0 11.4 %all-gather.3.cloned.1.call-done = f32[1024,512]{1,0:T(8,128)} async-done(((f32[128,512]{1,0:T(8,128)}), f32[1024,512]{1,0:T(8,128)}) %all-gather.3.cloned.1.call-update) | async-done | bytes 2097168 | tf_op jit(solution)/shard_map/all_gather | solution.py:39
  125.3 1.8 reduce_sum.9
  127.2 35.3 %reduce-scatter.4.cloned.1.call-done = f32[128,16]{0,1:T(8,128)} async-done(((f32[128,128]{0,1:T(8,128)}), f32[128,16]{0,1:T(8,128)}) %reduce-scatter.4.cloned.1.call-update) | async-done | bytes 8208 | tf_op jit(solution)/shard_map/reduce_scatter | solution.py:34
  162.5 1.0 fusion.3
  163.5 13.2 %all_gather.24 = f32[512,16]{0,1:T(8,128)S(1)} all-gather(f32[128,16]{0,1:T(8,128)S(1)} %fusion.3), channel_id=1, replica_groups=mesh['term'=8,'topic'=4] {'topic'}, dimensions={0}, use_global_device_ids=true | all-gather | bytes 40960 | tf_op jit(solution)/shard_map/all_gather | solution.py:20
  176.7 1.0 fusion.2
  177.7 13.1 %all_gather.25 = f32[512,16]{0,1:T(8,128)S(1)} all-gather(f32[128,16]{0,1:T(8,128)S(1)} %fusion.2), channel_id=1, replica_groups=mesh['term'=8,'topic'=4] {'topic'}, dimensions={0}, use_global_device_ids=true | all-gather | bytes 40960 | tf_op jit(solution)/shard_map/all_gather | solution.py:20
  190.8 1.0 fusion.1
  191.9 0.0 copy-start.3
  191.9 9.2 %all_gather.27 = f32[128,128]{0,1:T(8,128)S(1)} all-gather(f32[128,16]{0,1:T(8,128)S(1)} %fusion.1), channel_id=1, replica_groups=mesh['term'=8,'topic'=4] {'term'}, dimensions={1}, use_global_device_ids=true | all-gather | bytes 73728 | tf_op jit(solution)/shard_map/all_gather | solution.py:52
  201.1 13.1 %all_gather.26 = f32[512,16]{0,1:T(8,128)S(1)} all-gather(f32[128,16]{0,1:T(8,128)S(1)} %fusion.1), channel_id=1, replica_groups=mesh['term'=8,'topic'=4] {'topic'}, dimensions={0}, use_global_device_ids=true | all-gather | bytes 40960 | tf_op jit(solution)/shard_map/all_gather | solution.py:45
  214.2 1.3 fusion.8
  215.5 0.0 reduce-scatter.8.cloned.1.call-update
  215.5 0.0 copy-start.4
  215.6 7.4 %fusion = f32[8192,128]{1,0:T(8,128)} fusion(bf16[128,8192]{1,0:T(8,128)(2,1)} %copy-done.1, f32[128,128]{0,1:T(8,128)S(1)} %all_gather.27, f32[8192,128]{1,0:T(8,128)} %param.11), kind=kOutput, calls=%fused_computation.1 | convolution fusion | flops 1613758464 | bytes 10551296 | tf_op jit(solution)/shard_map/dot_general | solution.py:54
  222.9 0.0 copy-done.3
  222.9 26.5 %reduce-scatter.8.cloned.1.call-done = f32[128,64]{0,1:T(8,128)} async-done(((f32[128,512]{0,1:T(8,128)}), f32[128,64]{0,1:T(8,128)}) %reduce-scatter.8.cloned.1.call-update) | async-done | bytes 32784 | tf_op jit(solution)/shard_map/reduce_scatter | solution.py:50
  249.4 0.0 copy-done.4
  249.4 1.4 multiply_add_fusion
Async XLA Ops:
  7.2 90.1 %copy-start = (bf16[8192,128]{1,0:T(8,128)(2,1)S(1)}, bf16[8192,128]{1,0:T(8,128)(2,1)}, u32[]{:S(2)}) copy-start(bf16[8192,128]{1,0:T(8,128)(2,1)} %param.7) | copy-start | bytes 6291460
  7.2 90.0 %reduce-scatter.6.cloned.1.call-start = ((), (), s32[]{:S(2)}) async-start(), calls=%async_computation.5 | async-start | bytes 1310720 | tf_op jit(solution)/shard_map/reduce_scatter | solution.py:36
  66.0 31.3 %copy-start.6 = (s32[1,128]{1,0:T(1,128)S(1)}, s32[1,128]{1,0:T(1,128)}, u32[]{:S(2)}) copy-start(s32[1,128]{1,0:T(1,128)} %param.8) | copy-start | bytes 1540
  70.5 54.9 %all-gather.3.cloned.1.call-start = ((), (), s32[]{:S(2)}) async-start(), calls=%async_computation.7 | async-start | bytes 2359296 | tf_op jit(solution)/shard_map/all_gather | solution.py:39
  97.2 65.3 %reduce-scatter.4.cloned.1.call-start = ((), (), s32[]{:S(2)}) async-start(), calls=%async_computation.4 | async-start | bytes 73728 | tf_op jit(solution)/shard_map/reduce_scatter | solution.py:34
  97.2 2.2 copy-start.2
  98.1 1.3 copy-start.1
  99.4 1.4 copy-start.5
  100.8 148.6 %reduce-scatter.8.cloned.1.call-start = ((), (), s32[]{:S(2)}) async-start(), calls=%async_computation.6 | async-start | bytes 294912 | tf_op jit(solution)/shard_map/reduce_scatter | solution.py:50
  191.9 31.0 %copy-start.3 = (f32[128,16]{0,1:T(8,128)}, f32[128,16]{0,1:T(8,128)S(1)}, u32[]{:S(2)}) copy-start(f32[128,16]{0,1:T(8,128)S(1)} %fusion.1) | copy-start | bytes 24580
  215.5 33.8 %copy-start.4 = (f32[128,64]{0,1:T(8,128)S(1)}, f32[128,64]{0,1:T(8,128)}, u32[]{:S(2)}) copy-start(f32[128,64]{0,1:T(8,128)} %param.10) | copy-start | bytes 98308
Sparse Core Ops, SparseCore 0:
  70.6 26.5 reduce-scatter.5
  99.0 26.2 all-gather.2
  128.9 33.5 reduce-scatter.3
  215.7 33.6 reduce-scatter.7
